TPU v7x, 32 devices: a whole 2x2x4 slice. The times are simulated.
32 devices in a mesh: party: 2 (over x), dp: 16 (over z, y, core).
Axes of the slice: x: 2, y: 2, z: 4, core: 2. Of those that a mesh axis runs over, the one named last changes fastest.
Arguments:
- x_share: float32 [2, 8192, 1024], P('party', 'dp'), may hold values from -6 to 6
- w_share: float32 [2, 1024, 2048], P('party', 'dp'), may hold values from -0.1875 to 0.1875
- g_share: float32 [2, 8192, 2048], P('party', 'dp'), may hold values from -0.0625 to 0.0625
- fwd_a: float32 [2, 8192, 1024], P('party', 'dp'), may hold values from -4 to 4
- fwd_b: float32 [2, 1024, 2048], P('party', 'dp'), may hold values from -0.125 to 0.125
- fwd_c: float32 [2, 8192, 2048], P('party', 'dp'), may hold values from -2100 to 2100, as said below
- bwd_a: float32 [2, 8192, 1024], P('party', 'dp'), may hold values from -4 to 4
- bwd_b: float32 [2, 8192, 2048], P('party', 'dp'), may hold values from -0.044194174 to 0.044194174
- bwd_c: float32 [2, 1024, 2048], P('party', 'dp'), may hold values from -2100 to 2100, as said below
Outputs:
- y_share: float32 [2, 8192, 2048], P('party', 'dp')
- dw_share: float32 [2, 1024, 2048], P('party', 'dp')
Inputs may be any that keep to these rules, and one draw needn't show every extreme that they name: fwd_c[0] + fwd_c[1] equals (fwd_a[0] + fwd_a[1]) (fwd_b[0] + fwd_b[1]) up to float32 rounding. bwd_c[0] + bwd_c[1] equals (bwd_a[0] + bwd_a[1])^T (bwd_b[0] + bwd_b[1]) up to float32 rounding.
All inputs are finite; a program needn't handle non-finite values.
Results may differ from a plain program's by a relative error of at most 0.0001.
Values sent between devices are 32-bit elements; how exact they have to be, the bound alone decides.
A program may use at most 128 MiB of HBM per device.

v0:
```python
import functools

import jax
import jax.numpy as jnp
from jax import lax
from jax.experimental import pallas as pl
from jax.experimental.pallas import tpu as pltpu
from jax.sharding import PartitionSpec as P

MESH = pl.DeviceIdType.MESH
STREAMS = 4


def place(index, n):
    z, y, core = index // 4, (index // 2) % 2, index % 2
    return 2 * (z + y * (n // 2 - 1 - 2 * z)) + core


def index_at(spot, n):
    chip, core = spot // 2, spot % 2
    y = chip // (n // 4)
    z = chip + y * (n // 2 - 1 - 2 * chip)
    return 4 * z + 2 * y + core


def scatter_kernel(n, part_ref, base_ref, out_ref, own, slots, load_sem, send_sem, recv_sem):
    me = place(lax.axis_index("dp"), n)
    after, before = index_at(lax.rem(me + 1, n), n), index_at(lax.rem(me + n - 1, n), n)
    rows, columns = base_ref.shape
    width = columns // STREAMS
    load = pltpu.make_async_copy(part_ref, own, load_sem)
    load.start()
    barrier = pltpu.get_barrier_semaphore()
    for neighbour in (after, before):
        pl.semaphore_signal(barrier, inc=1, device_id={"dp": neighbour}, device_id_type=MESH)
    pl.semaphore_wait(barrier, 2)
    load.wait()

    def rows_of(sign, step):
        owner = index_at(lax.rem(me + sign * (n - 1 - step) + n * 2, n), n)
        return pl.ds(pl.multiple_of(owner * rows, 8), rows)

    def copy_of(stream, step, source):
        target = after if stream % 2 == 0 else before
        return pltpu.make_async_remote_copy(
            src_ref=source,
            dst_ref=slots.at[stream, step],
            send_sem=send_sem.at[stream, step],
            recv_sem=recv_sem.at[stream, step],
            device_id={"dp": target},
            device_id_type=MESH,
        )

    def sign_of(stream):
        return 1 if stream % 2 == 0 else -1

    def first_source(stream):
        return own.at[rows_of(sign_of(stream), 0), pl.ds(stream * width, width)]

    for stream in range(STREAMS):
        copy_of(stream, 0, first_source(stream)).start()

    def hop(step, carry):
        for stream in range(STREAMS):
            copy_of(stream, step - 1, slots.at[stream, step - 1]).wait_recv()
            slots[stream, step - 1] = slots[stream, step - 1] + own[rows_of(sign_of(stream), step), pl.ds(stream * width, width)]
            copy_of(stream, step, slots.at[stream, step - 1]).start()
        return carry

    lax.fori_loop(1, n - 1, hop, 0)
    for stream in range(STREAMS):
        cols = pl.ds(stream * width, width)
        copy_of(stream, n - 2, slots.at[stream, n - 2]).wait_recv()
        out_ref[:, cols] = base_ref[:, cols] + (slots[stream, n - 2] + own[rows_of(sign_of(stream), n - 1), cols])

    def drain(step, carry):
        for stream in range(STREAMS):
            copy_of(stream, step, slots.at[stream, step]).wait_send()
        return carry

    lax.fori_loop(0, n - 1, drain, 0)


def scatter_sum(part, base, n, number):
    rows, columns = base.shape
    return pl.pallas_call(
        functools.partial(scatter_kernel, n),
        out_shape=jax.ShapeDtypeStruct(base.shape, base.dtype),
        in_specs=[pl.BlockSpec(memory_space=pl.ANY), pl.BlockSpec(memory_space=pltpu.VMEM)],
        out_specs=pl.BlockSpec(memory_space=pltpu.VMEM),
        scratch_shapes=[
            pltpu.VMEM(part.shape, part.dtype),
            pltpu.VMEM((STREAMS, n - 1, rows, columns // STREAMS), part.dtype),
            pltpu.SemaphoreType.DMA,
            pltpu.SemaphoreType.DMA((STREAMS, n - 1)),
            pltpu.SemaphoreType.DMA((STREAMS, n - 1)),
        ],
        compiler_params=pltpu.CompilerParams(
            collective_id=number, has_side_effects=True, vmem_limit_bytes=40 * 1024 * 1024
        ),
        cost_estimate=pl.CostEstimate(flops=0, bytes_accessed=80 * 1024 * 1024, transcendentals=0),
    )(part, base)


def matmul(left, right):
    return jnp.dot(left, right, preferred_element_type=jnp.float32, precision=lax.Precision.HIGH)


def tmatmul(left, right):
    return lax.dot_general(
        left,
        right,
        (((0,), (0,)), ((), ())),
        precision=lax.Precision.HIGH,
        preferred_element_type=jnp.float32,
    )


def swap(value):
    return lax.ppermute(value, "party", [(0, 1), (1, 0)])


CUTS = 2


def body(n, x_share, w_share, g_share, fwd_a, fwd_b, fwd_c, bwd_a, bwd_b, bwd_c):
    first = (lax.axis_index("party") == 0).astype(jnp.float32)
    inputs, a_f, b_f, a_b, b_b = x_share[0], fwd_a[0], fwd_b[0], bwd_a[0], bwd_b[0]
    own_w = w_share[0] - b_f
    gathered_b = lax.all_gather(b_f, "dp", axis=0, tiled=True)
    got_w = swap(own_w)
    delta_fwd = lax.all_gather(own_w + got_w, "dp", axis=0, tiled=True)
    own_e = inputs - a_b
    got_e = swap(own_e)
    width = b_b.shape[1] // CUTS
    cuts = [slice(i * width, (i + 1) * width) for i in range(CUTS)]
    own_d = [g_share[0, :, c] - b_b[:, c] for c in cuts]
    got_d = [swap(d) for d in own_d]
    own_f = inputs - a_f
    half = own_f.shape[0] // 2
    got_f = [swap(own_f[:half]), swap(own_f[half:])]
    eps_bwd = own_e + got_e
    right = a_b + first * eps_bwd
    grads = []
    for i, c in enumerate(cuts):
        part = tmatmul(eps_bwd, b_b[:, c]) + tmatmul(right, own_d[i] + got_d[i])
        grads.append(scatter_sum(part, bwd_c[0, :, c], n, i))
    outputs = []
    for i, r in enumerate((slice(0, half), slice(half, None))):
        eps_fwd = own_f[r] + got_f[i]
        outputs.append(fwd_c[0, r] + matmul(eps_fwd, gathered_b) + matmul(a_f[r] + first * eps_fwd, delta_fwd))
    return (jnp.concatenate(outputs)[None], jnp.concatenate(grads, axis=1)[None])


def solution(mesh):
    spec = P("party", "dp", None)
    return jax.shard_map(
        functools.partial(body, mesh.shape["dp"]),
        mesh=mesh,
        in_specs=(spec,) * 9,
        out_specs=(spec, spec),
        check_vma=False,
    )
```

profile of v0, /device:TPU:0, one launch (start us, length us, event | category | flops | bytes accessed | tf_op | source)
XLA Modules:
  0.0 301.4 jit_solution(4040713394605944238)
XLA Ops:
  7.2 0.0 all-gather.4.cloned.1.call-start
  7.2 1.3 subtract_bitcast_fusion
  8.5 3.0 %collective-permute-start.1 = (f32[64,2048]{1,0:T(8,128)S(1)}, f32[64,2048]{1,0:T(8,128)S(1)}, u32[]{:S(2)}, u32[]{:S(2)}) collective-permute-start(f32[64,2048]{1,0:T(8,128)S(1)} %subtract_bitcast_fusion), channel_id=1, source_target_pairs={{0,16},{16,0},{1,17},{17,1},{2,18},{18,2},{3,19},{19,3},{4,20},{20... | collective-permute-start | bytes 1572872 | tf_op jit(solution)/shard_map/ppermute | solution.py:120
  11.5 11.9 %collective-permute-done.1 = f32[64,2048]{1,0:T(8,128)S(1)} collective-permute-done((f32[64,2048]{1,0:T(8,128)S(1)}, f32[64,2048]{1,0:T(8,128)S(1)}, u32[]{:S(2)}, u32[]{:S(2)}) %collective-permute-start.1) | collective-permute-done | bytes 524320 | tf_op jit(solution)/shard_map/ppermute | solution.py:120
  23.4 0.9 add.48
  24.3 0.0 all-gather.4.cloned.1.call-update
  24.3 0.0 all-gather.6.cloned.1.call-start
  24.4 0.7 all-gather.6.cloned.1.call-update
  25.1 0.0 copy-start.5
  25.1 0.0 copy-start.9
  25.1 3.7 %bitcast_subtract_fusion.2 = (f32[512,1024]{1,0:T(8,128)S(1)}, f32[512,1024]{1,0:T(8,128)S(1)}) fusion(f32[1,512,1024]{2,1,0:T(8,128)} %param.15, f32[1,512,1024]{2,1,0:T(8,128)} %param.9, f32[1,512,1024]{2,1,0:T(8,128)} %param.12), kind=kLoop, calls=%fused_computation.14 | loop fusion | flops 1048576 | bytes 10485760 | tf_op jit(solution)/shard_map/sub | solution.py:133
  28.8 0.0 copy-start.2
  28.8 1.8 collective-permute-start.3
  30.6 0.0 copy-done.5
  30.6 0.5 copy-done.9
  31.2 2.9 bitcast_subtract_fusion.1
  34.1 1.7 collective-permute-start.4
  35.8 0.3 collective-permute-start.5
  36.1 0.0 copy-done.2
  36.1 1.6 fusion.42
  37.7 1.7 collective-permute-start
  39.4 0.3 collective-permute-start.2
  39.7 1.1 slice_bitcast_fusion.1
  40.8 0.0 copy-start.6
  40.8 36.7 %collective-permute-done.3 = f32[512,1024]{1,0:T(8,128)} collective-permute-done((f32[512,1024]{1,0:T(8,128)S(1)}, f32[512,1024]{1,0:T(8,128)}, u32[]{:S(2)}, u32[]{:S(2)}) %collective-permute-start.3) | collective-permute-done | bytes 2097184 | tf_op jit(solution)/shard_map/ppermute | solution.py:120
  77.5 44.9 %collective-permute-done.4 = f32[512,1024]{1,0:T(8,128)} collective-permute-done((f32[512,1024]{1,0:T(8,128)}, f32[512,1024]{1,0:T(8,128)}, u32[]{:S(2)}, u32[]{:S(2)}) %collective-permute-start.4) | collective-permute-done | bytes 2097184 | tf_op jit(solution)/shard_map/ppermute | solution.py:120
  122.4 7.2 %fusion.18 = f32[1024,1024]{1,0:T(8,128)S(1)} fusion(f32[512,1024]{1,0:T(8,128)} %get-tuple-element.2, f32[512,1024]{1,0:T(8,128)} %collective-permute-done.4, f32[1,512,1024]{2,1,0:T(8,128)} %param.15, f32[]{:T(128)S(6)} %convert_element_type.3, f32[512,1024]{1,0:T(8,128)S(1)} %get-tuple-element.4, f32[512,1024]{1,0:T(8,128)} %collective-permute-done.3), kind=kOutput, calls=%fused_computation.18 | convolution fusion | flops 3223322624 | bytes 14680068 | tf_op jit(solution)/shard_map/dot_general | solution.py:110
  129.6 0.0 copy-done.6
  129.6 0.0 copy-start.4
  129.6 5.3 %convolution_add_fusion.1.part_ref = f32[1024,1024]{1,0:T(8,128)S(1)} fusion(f32[1024,1024]{1,0:T(8,128)S(1)} %fusion.18, f32[512,2048]{1,0:T(8,128)S(1)} %bitcast.51, f32[512,1024]{1,0:T(8,128)S(1)} %get-tuple-element.4, f32[512,1024]{1,0:T(8,128)} %collective-permute-done.3), kind=kOutput, calls=%fused_computation.10 | convolution fusion | flops 3222798336 | bytes 14680064 | tf_op jit(solution)/shard_map/dot_general | solution.py:110
  135.0 32.4 %collective-permute-done.5 = f32[512,1024]{1,0:T(8,128)} collective-permute-done((f32[512,1024]{1,0:T(8,128)}, f32[512,1024]{1,0:T(8,128)}, u32[]{:S(2)}, u32[]{:S(2)}) %collective-permute-start.5) | collective-permute-done | bytes 2097184 | tf_op jit(solution)/shard_map/ppermute | solution.py:120
  167.4 0.0 copy-done.4
  167.4 6.6 %fusion.16 = f32[1024,1024]{1,0:T(8,128)S(1)} fusion(f32[512,1024]{1,0:T(8,128)} %get-tuple-element.3, f32[512,1024]{1,0:T(8,128)} %collective-permute-done.5, f32[1,512,1024]{2,1,0:T(8,128)S(1)} %copy-done.4, f32[]{:T(128)S(6)} %convert_element_type.3, f32[512,1024]{1,0:T(8,128)S(1)} %get-tuple-element.4, f32[512,1024]{1,0:T(8,128)} %collective-permute-done.3), kind=kOutput, calls=%fused_computation.16 | convolution fusion | flops 3223322624 | bytes 14680068 | tf_op jit(solution)/shard_map/dot_general | solution.py:110
  174.0 5.2 %convolution_add_fusion.part_ref = f32[1024,1024]{1,0:T(8,128)S(1)} fusion(f32[1024,1024]{1,0:T(8,128)S(1)} %fusion.16, f32[512,2048]{1,0:T(8,128)S(1)} %bitcast.52, f32[512,1024]{1,0:T(8,128)S(1)} %get-tuple-element.4, f32[512,1024]{1,0:T(8,128)} %collective-permute-done.3), kind=kOutput, calls=%fused_computation.9 | convolution fusion | flops 3222798336 | bytes 14680064 | tf_op jit(solution)/shard_map/dot_general | solution.py:110
  179.2 40.4 %shard_map.104 = f32[64,1024]{1,0:T(8,128)S(1)} custom-call(f32[1024,1024]{1,0:T(8,128)S(1)} %convolution_add_fusion.1.part_ref, f32[64,1024]{1,0:T(8,128)S(1)} %get-tuple-element.8.base_ref), custom_call_target="tpu_custom_call" | custom-call | bytes 83886080 | tf_op jit(solution)/shard_map/pallas_call | solution.py:86
  219.6 0.0 copy-start.3
  219.6 39.8 %shard_map.105 = f32[64,1024]{1,0:T(8,128)S(1)} custom-call(f32[1024,1024]{1,0:T(8,128)S(1)} %convolution_add_fusion.part_ref, f32[64,1024]{1,0:T(8,128)S(1)} %get-tuple-element.9.base_ref), custom_call_target="tpu_custom_call" | custom-call | bytes 83886080 | tf_op jit(solution)/shard_map/pallas_call | solution.py:86
  259.4 0.8 maximum_bitcast_fusion.1
  260.2 0.0 collective-permute-done
  260.2 0.0 all-gather.4.cloned.1.call-done
  260.2 0.0 copy-done.3
  260.2 0.0 copy-start.1
  260.2 0.0 copy-start.7
  260.2 9.0 %fusion.23 = f32[256,2048]{1,0:T(8,128)} fusion(f32[1024,2048]{1,0:T(8,128)} %all-gather.4.cloned.1.call-done, f32[1,512,1024]{2,1,0:T(8,128)} %param.12, f32[]{:T(128)S(6)} %convert_element_type.3, f32[256,1024]{1,0:T(8,128)S(1)} %collective-permute-done, f32[512,1024]{1,0:T(8,128)S(1)} %copy-done.3), kind=kOutput, calls=%fused_computation.25 | convolution fusion | flops 3222011904 | bytes 13631492 | tf_op jit(solution)/shard_map/dot_general | solution.py:106
  269.2 0.0 collective-permute-done.2
  269.2 0.0 copy-done.1
  269.2 0.0 copy-done.7
  269.2 6.9 %fusion.22 = f32[256,2048]{1,0:T(8,128)} fusion(f32[1024,2048]{1,0:T(8,128)S(1)} %copy-done.1, f32[1,512,1024]{2,1,0:T(8,128)S(1)} %copy-done.7, f32[]{:T(128)S(6)} %convert_element_type.3, f32[256,1024]{1,0:T(8,128)} %collective-permute-done.2, f32[512,1024]{1,0:T(8,128)S(1)} %copy-done.3), kind=kOutput, calls=%fused_computation.23 | convolution fusion | flops 3222011904 | bytes 13631492 | tf_op jit(solution)/shard_map/dot_general | solution.py:106
  276.1 0.0 all-gather.6.cloned.1.call-done
  276.1 0.0 copy-start
  276.1 0.0 copy-start.8
  276.1 0.0 copy-start.10
  276.1 10.0 %fusion.7 = f32[256,2048]{1,0:T(8,128)S(1)} fusion(f32[256,2048]{1,0:T(8,128)} %fusion.23, f32[1,1024,2048]{2,1,0:T(8,128)} %all-gather.6.cloned.1.call-done, f32[1,512,2048]{2,1,0:T(8,128)} %param.14, f32[256,1024]{1,0:T(8,128)S(1)} %collective-permute-done, f32[512,1024]{1,0:T(8,128)S(1)} %copy-done.3), kind=kOutput, calls=%fused_computation.6 | convolution fusion | flops 3222536192 | bytes 16777216 | tf_op jit(solution)/shard_map/dot_general | solution.py:106
  286.2 0.0 copy-done
  286.2 0.0 copy-done.8
  286.2 0.0 copy-done.10
  286.2 5.8 %fusion.13 = f32[256,2048]{1,0:T(8,128)S(1)} fusion(f32[256,2048]{1,0:T(8,128)S(1)} %copy-done.8, f32[1,1024,2048]{2,1,0:T(8,128)S(1)} %copy-done, f32[1,512,2048]{2,1,0:T(8,128)S(1)} %copy-done.10, f32[256,1024]{1,0:T(8,128)} %collective-permute-done.2, f32[512,1024]{1,0:T(8,128)S(1)} %copy-done.3), kind=kOutput, calls=%fused_computation.8 | convolution fusion | flops 3222536192 | bytes 16777216 | tf_op jit(solution)/shard_map/dot_general | solution.py:106
  292.0 2.5 maximum_bitcast_fusion
Async XLA Ops:
  7.2 253.1 %all-gather.4.cloned.1.call-start = ((), (), s32[]{:S(2)}) async-start(), calls=%async_computation | async-start | bytes 8912896 | tf_op jit(solution)/shard_map/all_gather | solution.py:132
  8.5 15.0 %collective-permute-start.1 = (f32[64,2048]{1,0:T(8,128)S(1)}, f32[64,2048]{1,0:T(8,128)S(1)}, u32[]{:S(2)}, u32[]{:S(2)}) collective-permute-start(f32[64,2048]{1,0:T(8,128)S(1)} %subtract_bitcast_fusion), channel_id=1, source_target_pairs={{0,16},{16,0},{1,17},{17,1},{2,18},{18,2},{3,19},{19,3},{4,20},{20... | collective-permute-start | bytes 1572872 | tf_op jit(solution)/shard_map/ppermute | solution.py:120
  24.3 251.8 %all-gather.6.cloned.1.call-start = ((), (), s32[]{:S(2)}) async-start(), calls=%async_computation.1 | async-start | bytes 8912896 | tf_op jit(solution)/shard_map/all_gather | solution.py:130
  25.1 5.6 %copy-start.5 = (f32[1,512,2048]{2,1,0:T(8,128)S(1)}, f32[1,512,2048]{2,1,0:T(8,128)}, u32[]{:S(2)}) copy-start(f32[1,512,2048]{2,1,0:T(8,128)} %param.16) | copy-start | bytes 12582916
  25.1 6.1 %copy-start.9 = (f32[1,512,2048]{2,1,0:T(8,128)S(1)}, f32[1,512,2048]{2,1,0:T(8,128)}, u32[]{:S(2)}) copy-start(f32[1,512,2048]{2,1,0:T(8,128)} %param.11) | copy-start | bytes 12582916
  28.8 7.3 %copy-start.2 = (f32[512,1024]{1,0:T(8,128)}, f32[512,1024]{1,0:T(8,128)S(1)}, u32[]{:S(2)}) copy-start(f32[512,1024]{1,0:T(8,128)S(1)} %get-tuple-element.5) | copy-start | bytes 6291460
  28.8 48.7 %collective-permute-start.3 = (f32[512,1024]{1,0:T(8,128)S(1)}, f32[512,1024]{1,0:T(8,128)}, u32[]{:S(2)}, u32[]{:S(2)}) collective-permute-start(f32[512,1024]{1,0:T(8,128)S(1)} %get-tuple-element.4), channel_id=1, source_target_pairs={{0,16},{16,0},{1,17},{17,1},{2,18},{18,2},{3,19},{19,3},{4,20},{20... | collective-permute-start | bytes 6291464 | tf_op jit(solution)/shard_map/ppermute | solution.py:120
  34.1 88.3 %collective-permute-start.4 = (f32[512,1024]{1,0:T(8,128)}, f32[512,1024]{1,0:T(8,128)}, u32[]{:S(2)}, u32[]{:S(2)}) collective-permute-start(f32[512,1024]{1,0:T(8,128)} %get-tuple-element.2), channel_id=1, source_target_pairs={{0,16},{16,0},{1,17},{17,1},{2,18},{18,2},{3,19},{19,3},{4,20},{20... | collective-permute-start | bytes 6291464 | tf_op jit(solution)/shard_map/ppermute | solution.py:120
  35.8 131.5 %collective-permute-start.5 = (f32[512,1024]{1,0:T(8,128)}, f32[512,1024]{1,0:T(8,128)}, u32[]{:S(2)}, u32[]{:S(2)}) collective-permute-start(f32[512,1024]{1,0:T(8,128)} %get-tuple-element.3), channel_id=1, source_target_pairs={{0,16},{16,0},{1,17},{17,1},{2,18},{18,2},{3,19},{19,3},{4,20},{20... | collective-permute-start | bytes 6291464 | tf_op jit(solution)/shard_map/ppermute | solution.py:120
  37.7 222.5 %collective-permute-start = (f32[256,1024]{1,0:T(8,128)}, f32[256,1024]{1,0:T(8,128)S(1)}, u32[]{:S(2)}, u32[]{:S(2)}) collective-permute-start(f32[256,1024]{1,0:T(8,128)} %get-tuple-element.6), channel_id=1, source_target_pairs={{0,16},{16,0},{1,17},{17,1},{2,18},{18,2},{3,19},{19,3},{4,20},{20... | collective-permute-start | bytes 3145736 | tf_op jit(solution)/shard_map/ppermute | solution.py:120
  39.4 229.8 %collective-permute-start.2 = (f32[256,1024]{1,0:T(8,128)}, f32[256,1024]{1,0:T(8,128)}, u32[]{:S(2)}, u32[]{:S(2)}) collective-permute-start(f32[256,1024]{1,0:T(8,128)} %get-tuple-element.7), channel_id=1, source_target_pairs={{0,16},{16,0},{1,17},{17,1},{2,18},{18,2},{3,19},{19,3},{4,20},{20... | collective-permute-start | bytes 3145736 | tf_op jit(solution)/shard_map/ppermute | solution.py:120
  40.8 88.8 %copy-start.6 = (f32[1,512,2048]{2,1,0:T(8,128)S(1)}, f32[1,512,2048]{2,1,0:T(8,128)}, u32[]{:S(2)}) copy-start(f32[1,512,2048]{2,1,0:T(8,128)} %param.16) | copy-start | bytes 12582916
  129.6 37.7 %copy-start.4 = (f32[1,512,1024]{2,1,0:T(8,128)S(1)}, f32[1,512,1024]{2,1,0:T(8,128)}, u32[]{:S(2)}) copy-start(f32[1,512,1024]{2,1,0:T(8,128)} %param.15) | copy-start | bytes 6291460
  219.6 40.7 %copy-start.3 = (f32[512,1024]{1,0:T(8,128)S(1)}, f32[512,1024]{1,0:T(8,128)}, u32[]{:S(2)}) copy-start(f32[512,1024]{1,0:T(8,128)} %copy-done.2) | copy-start | bytes 6291460
  260.2 9.0 %copy-start.1 = (f32[1024,2048]{1,0:T(8,128)S(1)}, f32[1024,2048]{1,0:T(8,128)}, u32[]{:S(2)}) copy-start(f32[1024,2048]{1,0:T(8,128)} %all-gather.4.cloned.1.call-done) | copy-start | bytes 25165828
  260.2 9.0 %copy-start.7 = (f32[1,512,1024]{2,1,0:T(8,128)S(1)}, f32[1,512,1024]{2,1,0:T(8,128)}, u32[]{:S(2)}) copy-start(f32[1,512,1024]{2,1,0:T(8,128)} %param.12) | copy-start | bytes 6291460
  276.1 10.0 %copy-start = (f32[1,1024,2048]{2,1,0:T(8,128)S(1)}, f32[1,1024,2048]{2,1,0:T(8,128)}, u32[]{:S(2)}) copy-start(f32[1,1024,2048]{2,1,0:T(8,128)} %all-gather.6.cloned.1.call-done) | copy-start | bytes 25165828
  276.1 10.0 %copy-start.8 = (f32[256,2048]{1,0:T(8,128)S(1)}, f32[256,2048]{1,0:T(8,128)}, u32[]{:S(2)}) copy-start(f32[256,2048]{1,0:T(8,128)} %fusion.22) | copy-start | bytes 6291460
  276.1 10.0 %copy-start.10 = (f32[1,512,2048]{2,1,0:T(8,128)S(1)}, f32[1,512,2048]{2,1,0:T(8,128)}, u32[]{:S(2)}) copy-start(f32[1,512,2048]{2,1,0:T(8,128)} %param.14) | copy-start | bytes 12582916
Sparse Core Ops, SparseCore 0:
  24.4 75.7 all-gather.3
  102.4 72.8 all-gather.5
where the time goes:
time: 302 us; the launch traced here: 301 us
  waiting for transfers between devices  127 us (42%)
  Pallas kernels  80.2 us (27%)
  matrix products  56 us (19%)
  between operations  14.2 us (5%)
  other arithmetic  12.1 us (4%)
  starting transfers between devices  8.97 us (3%)
  local copies, waits for them, and re-layouts  3.24 us (1%)
    ppermute x6, waiting for transfers between devices, swap(): return lax.ppermute(value, 'party', [(0, 1), (1, 0)])  126 us
    pallas_call x2, Pallas kernels, scatter_sum(): pl.pallas_call(functools.partial(scatter_kernel, n), out_shape=jax.ShapeD...  80.2 us
    dot_general x4, matrix products, matmul(): jnp.dot(left, right, preferred_element_type=jnp.float32, precision=lax.Pr...  31.7 us
    dot_general x4, matrix products, tmatmul(): lax.dot_general(left, right, (((0,), (0,)), ((), ())), precision=lax.Prec...  24.3 us
    ppermute x6, starting transfers between devices, swap(): return lax.ppermute(value, 'party', [(0, 1), (1, 0)])  8.89 us
  transfers between devices with their start and end apart: 8, of which 4 were waited for; matrix products, arithmetic and copies ran while one was open for 17% of the time, Pallas kernels for 27%

commit v1 on v0

v1 whole, which is shorter than its diff:
```python
import functools

import jax
import jax.numpy as jnp
from jax import lax
from jax.experimental import pallas as pl
from jax.experimental.pallas import tpu as pltpu
from jax.sharding import PartitionSpec as P


MESH = pl.DeviceIdType.MESH


def place(index, n):
    z, y, core = index // 4, (index // 2) % 2, index % 2
    return 2 * (z + y * (n // 2 - 1 - 2 * z)) + core


def index_at(spot, n):
    chip, core = spot // 2, spot % 2
    y = chip // (n // 4)
    z = chip + y * (n // 2 - 1 - 2 * chip)
    return 4 * z + 2 * y + core


def gather_kernel(n, own_ref, out_ref, keep_sem, send_sem, recv_sem):
    me = place(lax.axis_index("dp"), n)
    after, before = index_at(lax.rem(me + 1, n), n), index_at(lax.rem(me + n - 1, n), n)
    rows, columns = own_ref.shape
    width = columns // 2
    barrier = pltpu.get_barrier_semaphore()
    for neighbour in (after, before):
        pl.semaphore_signal(barrier, inc=1, device_id={"dp": neighbour}, device_id_type=MESH)
    pl.semaphore_wait(barrier, 2)

    def rows_of(sign, step):
        owner = index_at(lax.rem(me - sign * step + n, n), n)
        return pl.ds(pl.multiple_of(owner * rows, 8), rows)

    def copy_of(stream, step, start=False):
        sign = 1 if stream < 2 else -1
        cols = pl.ds((stream % 2) * width, width)
        here = out_ref.at[rows_of(sign, step), cols]
        return pltpu.make_async_remote_copy(
            src_ref=own_ref.at[:, cols] if start else here,
            dst_ref=here,
            send_sem=send_sem.at[stream, step],
            recv_sem=recv_sem.at[stream, step],
            device_id={"dp": after if stream < 2 else before},
            device_id_type=MESH,
        )

    def arrived(stream, step):
        sign = 1 if stream < 2 else -1
        cols = pl.ds((stream % 2) * width, width)
        here = out_ref.at[rows_of(sign, step + 1), cols]
        pltpu.make_async_remote_copy(
            src_ref=here,
            dst_ref=here,
            send_sem=send_sem.at[stream, step],
            recv_sem=recv_sem.at[stream, step],
            device_id={"dp": after if stream < 2 else before},
            device_id_type=MESH,
        ).wait_recv()

    up, down = n // 2, n - 1 - n // 2
    order = (0, 2, 1, 3)
    for stream in order:
        copy_of(stream, 0, True).start()
    keep = pltpu.make_async_copy(own_ref, out_ref.at[rows_of(1, 0)], keep_sem)
    keep.start()

    def hop(step, carry):
        for stream in order:
            arrived(stream, step - 1)
            copy_of(stream, step).start()
        return carry

    lax.fori_loop(1, down, hop, 0)
    for stream in (0, 1):
        arrived(stream, up - 2)
        copy_of(stream, up - 1).start()
    for stream in (2, 3):
        arrived(stream, down - 1)
    for stream in (0, 1):
        arrived(stream, up - 1)
    keep.wait()
    for stream in order:
        copy_of(stream, 0, True).wait_send()

    def drain(step, carry):
        for stream in order:
            copy_of(stream, step).wait_send()
        return carry

    lax.fori_loop(1, down, drain, 0)
    for stream in (0, 1):
        copy_of(stream, up - 1).wait_send()


def gather(own, n):
    rows, columns = own.shape
    return pl.pallas_call(
        functools.partial(gather_kernel, n),
        out_shape=jax.ShapeDtypeStruct((n * rows, columns), own.dtype),
        in_specs=[pl.BlockSpec(memory_space=pltpu.VMEM)],
        out_specs=pl.BlockSpec(memory_space=pl.ANY),
        scratch_shapes=[
            pltpu.SemaphoreType.DMA,
            pltpu.SemaphoreType.DMA((4, n // 2)),
            pltpu.SemaphoreType.DMA((4, n // 2)),
        ],
        compiler_params=pltpu.CompilerParams(
            collective_id=0, has_side_effects=True, vmem_limit_bytes=8 * 1024 * 1024
        ),
        cost_estimate=pl.CostEstimate(flops=0, bytes_accessed=160 * 1024 * 1024, transcendentals=0),
    )(own)


def matmul(left, right):
    return jnp.dot(left, right, preferred_element_type=jnp.float32, precision=lax.Precision.HIGH)


def tmatmul(left, right):
    return lax.dot_general(
        left,
        right,
        (((0,), (0,)), ((), ())),
        precision=lax.Precision.HIGH,
        preferred_element_type=jnp.float32,
    )


def swap(value):
    return lax.ppermute(value, "party", [(0, 1), (1, 0)])


CUTS = 4


def body(n, x_share, w_share, g_share, fwd_a, fwd_b, fwd_c, bwd_a, bwd_b, bwd_c):
    first = (lax.axis_index("party") == 0).astype(jnp.float32)
    inputs, a_f, b_f, a_b, b_b = x_share[0], fwd_a[0], fwd_b[0], bwd_a[0], bwd_b[0]
    own_w = w_share[0] - b_f
    gathered_b = lax.all_gather(b_f, "dp", axis=0, tiled=True)
    got_w = swap(own_w)
    delta_fwd = gather(own_w + got_w, n)
    own_e = inputs - a_b
    got_e = swap(own_e)
    width = b_b.shape[1] // CUTS
    cuts = [slice(i * width, (i + 1) * width) for i in range(CUTS)]
    own_d = [g_share[0, :, c] - b_b[:, c] for c in cuts]
    got_d = [swap(d) for d in own_d]
    own_f = inputs - a_f
    got_f = swap(own_f)
    own_e, delta_fwd = lax.optimization_barrier((own_e, delta_fwd))
    eps_bwd = own_e + got_e
    right = a_b + first * eps_bwd
    grads = []
    for i, c in enumerate(cuts):
        part = tmatmul(eps_bwd, b_b[:, c]) + tmatmul(right, own_d[i] + got_d[i])
        summed = lax.psum_scatter(part, "dp", scatter_dimension=0, tiled=True)
        grads.append(bwd_c[0, :, c] + summed)
    eps_fwd = own_f + got_f
    outputs = fwd_c[0] + matmul(eps_fwd, gathered_b) + matmul(a_f + first * eps_fwd, delta_fwd)
    return (outputs[None], jnp.concatenate(grads, axis=1)[None])


def solution(mesh):
    spec = P("party", "dp", None)
    return jax.shard_map(
        functools.partial(body, mesh.shape["dp"]),
        mesh=mesh,
        in_specs=(spec,) * 9,
        out_specs=(spec, spec),
        check_vma=False,
    )
```

time: 302 us -> 521 us (1.73)
  waiting for transfers between devices: 127 us -> 373 us
  Pallas kernels: 80.2 us -> 48.8 us
    reduce_scatter x0 -> x4, waiting for transfers between devices: none -> 159 us  [body(): summed = lax.psum_scatter(part, 'dp', scatter_dimension=0, tiled=True)]
    all_gather x1, waiting for transfers between devices: 0.01 us -> 73.3 us  [body(): gathered_b = lax.all_gather(b_f, 'dp', axis=0, tiled=True)]
    pallas_call x2 -> x1, Pallas kernels: 80.2 us -> 48.8 us  [gather(): pl.pallas_call(functools.partial(gather_kernel, n), out_shape=jax.ShapeDt...]
    ppermute x6 -> x7, waiting for transfers between devices: 126 us -> 140 us  [swap(): return lax.ppermute(value, 'party', [(0, 1), (1, 0)])]
    dot_general x4 -> x8, matrix products: 24.3 us -> 33.3 us  [tmatmul(): lax.dot_general(left, right, (((0,), (0,)), ((), ())), precision=lax.Prec...]
    dot_general x4 -> x2, matrix products: 31.7 us -> 23 us  [matmul(): jnp.dot(left, right, preferred_element_type=jnp.float32, precision=lax.Pr...]
    ppermute x6 -> x7, starting transfers between devices: 8.89 us -> 11.1 us  [swap(): return lax.ppermute(value, 'party', [(0, 1), (1, 0)])]
  transfers between devices with their start and end apart: 8 -> 12, of which waited for: 4 -> 8; matrix products, arithmetic and copies ran while one was open for 17% -> 6% of each run, Pallas kernels for 27% -> 9%
where the time goes in v1:
time: 521 us
  waiting for transfers between devices  373 us (72%)
  matrix products  56.3 us (11%)
  Pallas kernels  48.8 us (9%)
  other arithmetic  13.9 us (3%)
  between operations  13.9 us (3%)
  starting transfers between devices  11.7 us (2%)
    reduce_scatter x4, waiting for transfers between devices, body(): summed = lax.psum_scatter(part, 'dp', scatter_dimension=0, tiled=True)  159 us
    ppermute x7, waiting for transfers between devices, swap(): return lax.ppermute(value, 'party', [(0, 1), (1, 0)])  140 us
    all_gather x1, waiting for transfers between devices, body(): gathered_b = lax.all_gather(b_f, 'dp', axis=0, tiled=True)  73.3 us
    pallas_call x1, Pallas kernels, gather(): pl.pallas_call(functools.partial(gather_kernel, n), out_shape=jax.ShapeDt...  48.8 us
    dot_general x8, matrix products, tmatmul(): lax.dot_general(left, right, (((0,), (0,)), ((), ())), precision=lax.Prec...  33.3 us
    dot_general x2, matrix products, matmul(): jnp.dot(left, right, preferred_element_type=jnp.float32, precision=lax.Pr...  23 us
    ppermute x7, starting transfers between devices, swap(): return lax.ppermute(value, 'party', [(0, 1), (1, 0)])  11.1 us
  transfers between devices with their start and end apart: 12, of which 8 were waited for; matrix products, arithmetic and copies ran while one was open for 6% of the time, Pallas kernels for 9%

profile of v1, /device:TPU:0, one launch (start us, length us, event | category | flops | bytes accessed | tf_op | source)
XLA Modules:
  0.0 520.9 jit_solution(421726384961023995)
XLA Ops:
  7.2 0.0 reduce-scatter.5.cloned.1.call-start
  7.2 0.0 copy-start.2
  7.2 0.0 copy-start.7
  7.2 5.2 %bitcast_subtract_fusion = (f32[512,1024]{1,0:T(8,128)S(1)}, f32[512,1024]{1,0:T(8,128)}) fusion(f32[1,512,1024]{2,1,0:T(8,128)} %param.15, f32[1,512,1024]{2,1,0:T(8,128)} %param.9, f32[1,512,1024]{2,1,0:T(8,128)} %param.12), kind=kLoop, calls=%fused_computation.6 | loop fusion | flops 1048576 | bytes 10485760 | tf_op jit(solution)/shard_map/sub | solution.py:148
  12.5 3.0 collective-permute-start.2
  15.4 0.0 copy-done.2
  15.4 0.0 copy-done.7
  15.4 2.3 bitcast_subtract_fusion.5
  17.7 0.0 copy-done.5
  17.7 0.9 collective-permute-start.3
  18.6 0.0 copy-done.9
  18.6 0.0 copy-done.10
  18.6 0.9 subtract_bitcast_fusion
  19.4 1.2 collective-permute-start.1
  20.6 74.3 %collective-permute-done.1 = f32[64,2048]{1,0:T(8,128)} collective-permute-done((f32[64,2048]{1,0:T(8,128)}, f32[64,2048]{1,0:T(8,128)}, u32[]{:S(2)}, u32[]{:S(2)}) %collective-permute-start.1) | collective-permute-done | bytes 524320 | tf_op jit(solution)/shard_map/ppermute | solution.py:135
  94.9 1.3 add.68.own_ref
  96.1 0.0 copy-start.4
  96.1 0.0 copy-start.6
  96.1 48.8 %shard_map.104 = f32[1024,2048]{1,0:T(8,128)S(1)} custom-call(f32[64,2048]{1,0:T(8,128)S(1)} %add.68.own_ref), custom_call_target="tpu_custom_call" | custom-call | bytes 167772160 | tf_op jit(solution)/shard_map/pallas_call | solution.py:103
  144.9 0.0 copy-start
  144.9 3.3 copy-done
  148.2 0.0 collective-permute-done.2
  148.2 0.0 copy-done.4
  148.2 0.0 copy-done.6
  148.2 2.3 bitcast_add_fusion.1
  150.5 0.0 copy-start.1
  150.6 0.0 collective-permute-done.3
  150.6 4.2 fusion.12
  154.7 0.0 copy-done.1
  154.8 4.5 convolution_add_fusion.3
  159.2 0.0 reduce-scatter.5.cloned.1.call-update
  159.2 0.0 reduce-scatter.7.cloned.1.call-start
  159.3 1.7 collective-permute-start.4
  161.0 22.9 %collective-permute-done.4 = f32[512,512]{1,0:T(8,128)S(1)} collective-permute-done((f32[512,512]{1,0:T(8,128)}, f32[512,512]{1,0:T(8,128)S(1)}, u32[]{:S(2)}, u32[]{:S(2)}) %collective-permute-start.4) | collective-permute-done | bytes 1048608 | tf_op jit(solution)/shard_map/ppermute | solution.py:135
  183.9 3.7 fusion.10
  187.7 4.6 convolution_add_fusion.2
  192.3 0.0 reduce-scatter.7.cloned.1.call-update
  192.3 0.2 reduce-scatter.11.cloned.1.call-start
  192.5 1.6 collective-permute-start.6
  194.2 22.0 %collective-permute-done.6 = f32[512,512]{1,0:T(8,128)S(1)} collective-permute-done((f32[512,512]{1,0:T(8,128)}, f32[512,512]{1,0:T(8,128)S(1)}, u32[]{:S(2)}, u32[]{:S(2)}) %collective-permute-start.6) | collective-permute-done | bytes 1048608 | tf_op jit(solution)/shard_map/ppermute | solution.py:135
  216.2 3.7 fusion.6
  219.9 4.5 convolution_add_fusion
  224.5 0.0 reduce-scatter.11.cloned.1.call-update
  224.5 0.0 reduce-scatter.9.cloned.1.call-start
  224.5 1.4 collective-permute-start.5
  226.0 21.1 %collective-permute-done.5 = f32[512,512]{1,0:T(8,128)S(1)} collective-permute-done((f32[512,512]{1,0:T(8,128)S(1)}, f32[512,512]{1,0:T(8,128)S(1)}, u32[]{:S(2)}, u32[]{:S(2)}) %collective-permute-start.5) | collective-permute-done | bytes 1048608 | tf_op jit(solution)/shard_map/ppermute | solution.py:135
  247.1 3.5 fusion.8
  250.6 4.5 convolution_add_fusion.1
  255.1 0.0 reduce-scatter.9.cloned.1.call-update
  255.2 0.3 all-gather.3.cloned.1.call-start
  255.4 0.3 all-gather.3.cloned.1.call-update
  255.8 1.4 collective-permute-start
  257.1 30.0 %reduce-scatter.7.cloned.1.call-done = f32[64,512]{1,0:T(8,128)} async-done(((f32[1024,512]{1,0:T(8,128)}), f32[64,512]{1,0:T(8,128)}) %reduce-scatter.7.cloned.1.call-update) | async-done | bytes 131088 | tf_op jit(solution)/shard_map/reduce_scatter | solution.py:162
  287.1 64.5 %reduce-scatter.11.cloned.1.call-done = f32[64,512]{1,0:T(8,128)} async-done(((f32[1024,512]{1,0:T(8,128)}), f32[64,512]{1,0:T(8,128)}) %reduce-scatter.11.cloned.1.call-update) | async-done | bytes 131088 | tf_op jit(solution)/shard_map/reduce_scatter | solution.py:162
  351.6 64.4 %reduce-scatter.9.cloned.1.call-done = f32[64,512]{1,0:T(8,128)} async-done(((f32[1024,512]{1,0:T(8,128)}), f32[64,512]{1,0:T(8,128)}) %reduce-scatter.9.cloned.1.call-update) | async-done | bytes 131088 | tf_op jit(solution)/shard_map/reduce_scatter | solution.py:162
  416.1 0.0 copy-done.11
  416.1 1.2 bitcast_add_fusion.9
  417.2 0.8 maximum_bitcast_fusion
  418.1 0.0 collective-permute-done
  418.1 73.3 %all-gather.3.cloned.1.call-done = f32[1,1024,2048]{2,1,0:T(8,128)} async-done(((f32[1,64,2048]{2,1,0:T(8,128)}), f32[1,1024,2048]{2,1,0:T(8,128)}) %all-gather.3.cloned.1.call-update) | async-done | bytes 8388624 | tf_op jit(solution)/shard_map/all_gather | solution.py:145
  491.3 10.7 %fusion = f32[512,2048]{1,0:T(8,128)S(1)} fusion(f32[1,1024,2048]{2,1,0:T(8,128)} %all-gather.3.cloned.1.call-done, f32[512,1024]{1,0:T(8,128)} %get-tuple-element.13, f32[512,1024]{1,0:T(8,128)} %collective-permute-done), kind=kOutput, calls=%fused_computation | convolution fusion | flops 6442975232 | bytes 16777216 | tf_op jit(solution)/shard_map/dot_general | solution.py:121
  502.1 0.0 copy-done.3
  502.1 0.0 copy-done.8
  502.1 12.3 %fusion.3 = f32[1,512,2048]{2,1,0:T(8,128)} fusion(f32[512,2048]{1,0:T(8,128)S(1)} %fusion, f32[1,512,2048]{2,1,0:T(8,128)S(1)} %copy-done.8, f32[1024,2048]{1,0:T(8,128)} %copy-done, f32[1,512,1024]{2,1,0:T(8,128)S(1)} %copy-done.3, f32[]{:T(128)S(6)} %convert_element_type.3, f32[512,1024]{1,0:T(8,128)} %get-tuple-element.13, ...), kind=kOutput, calls=%fused_computation.4 | convolution fusion | flops 6446120960 | bytes 27262980 | tf_op jit(solution)/shard_map/dot_general | solution.py:121
  (7 shorter events, 0.0 us)
Async XLA Ops:
  7.2 250.0 %reduce-scatter.5.cloned.1.call-start = ((), (), s32[]{:S(2)}) async-start(), calls=%async_computation.4 | async-start | bytes 2228224 | tf_op jit(solution)/shard_map/reduce_scatter | solution.py:162
  7.2 8.2 %copy-start.2 = (f32[1,512,2048]{2,1,0:T(8,128)S(1)}, f32[1,512,2048]{2,1,0:T(8,128)}, u32[]{:S(2)}) copy-start(f32[1,512,2048]{2,1,0:T(8,128)} %param.16) | copy-start | bytes 12582916
  7.2 8.2 %copy-start.7 = (f32[1,512,2048]{2,1,0:T(8,128)S(1)}, f32[1,512,2048]{2,1,0:T(8,128)}, u32[]{:S(2)}) copy-start(f32[1,512,2048]{2,1,0:T(8,128)} %param.11) | copy-start | bytes 12582916
  12.4 5.3 %copy-start.5 = (f32[512,1024]{1,0:T(8,128)}, f32[512,1024]{1,0:T(8,128)S(1)}, u32[]{:S(2)}) copy-start(f32[512,1024]{1,0:T(8,128)S(1)} %get-tuple-element.5) | copy-start | bytes 6291460
  12.5 135.8 %collective-permute-start.2 = (f32[512,1024]{1,0:T(8,128)S(1)}, f32[512,1024]{1,0:T(8,128)}, u32[]{:S(2)}, u32[]{:S(2)}) collective-permute-start(f32[512,1024]{1,0:T(8,128)S(1)} %get-tuple-element.5), channel_id=1, source_target_pairs={{0,16},{16,0},{1,17},{17,1},{2,18},{18,2},{3,19},{19,3},{4,20},{20... | collective-permute-start | bytes 6291464 | tf_op jit(solution)/shard_map/ppermute | solution.py:135
  15.4 3.2 copy-start.9
  15.4 3.2 copy-start.10
  17.7 132.8 %collective-permute-start.3 = (f32[512,512]{1,0:T(8,128)}, f32[512,512]{1,0:T(8,128)}, u32[]{:S(2)}, u32[]{:S(2)}) collective-permute-start(f32[512,512]{1,0:T(8,128)} %get-tuple-element.8), channel_id=1, source_target_pairs={{0,16},{16,0},{1,17},{17,1},{2,18},{18,2},{3,19},{19,3},{4,20},{20... | collective-permute-start | bytes 3145736 | tf_op jit(solution)/shard_map/ppermute | solution.py:135
  19.4 75.4 %collective-permute-start.1 = (f32[64,2048]{1,0:T(8,128)}, f32[64,2048]{1,0:T(8,128)}, u32[]{:S(2)}, u32[]{:S(2)}) collective-permute-start(f32[64,2048]{1,0:T(8,128)} %subtract_bitcast_fusion), channel_id=1, source_target_pairs={{0,16},{16,0},{1,17},{17,1},{2,18},{18,2},{3,19},{19,3},{4,20},{20... | collective-permute-start | bytes 1572872 | tf_op jit(solution)/shard_map/ppermute | solution.py:135
  96.1 52.1 %copy-start.4 = (f32[1,512,1024]{2,1,0:T(8,128)S(1)}, f32[1,512,1024]{2,1,0:T(8,128)}, u32[]{:S(2)}) copy-start(f32[1,512,1024]{2,1,0:T(8,128)} %param.15) | copy-start | bytes 6291460
  96.1 52.1 %copy-start.6 = (f32[512,1024]{1,0:T(8,128)S(1)}, f32[512,1024]{1,0:T(8,128)}, u32[]{:S(2)}) copy-start(f32[512,1024]{1,0:T(8,128)} %copy-done.5) | copy-start | bytes 6291460
  144.9 3.3 copy-start
  150.5 4.2 copy-start.1
  159.2 127.8 %reduce-scatter.7.cloned.1.call-start = ((), (), s32[]{:S(2)}) async-start(), calls=%async_computation.5 | async-start | bytes 2228224 | tf_op jit(solution)/shard_map/reduce_scatter | solution.py:162
  159.3 24.6 %collective-permute-start.4 = (f32[512,512]{1,0:T(8,128)}, f32[512,512]{1,0:T(8,128)S(1)}, u32[]{:S(2)}, u32[]{:S(2)}) collective-permute-start(f32[512,512]{1,0:T(8,128)} %get-tuple-element.9), channel_id=1, source_target_pairs={{0,16},{16,0},{1,17},{17,1},{2,18},{18,2},{3,19},{19,3},{4,20},{20... | collective-permute-start | bytes 3145736 | tf_op jit(solution)/shard_map/ppermute | solution.py:135
  192.3 159.3 %reduce-scatter.11.cloned.1.call-start = ((), (), s32[]{:S(2)}) async-start(), calls=%async_computation.7 | async-start | bytes 2228224 | tf_op jit(solution)/shard_map/reduce_scatter | solution.py:162
  192.5 23.6 %collective-permute-start.6 = (f32[512,512]{1,0:T(8,128)}, f32[512,512]{1,0:T(8,128)S(1)}, u32[]{:S(2)}, u32[]{:S(2)}) collective-permute-start(f32[512,512]{1,0:T(8,128)} %get-tuple-element.10), channel_id=1, source_target_pairs={{0,16},{16,0},{1,17},{17,1},{2,18},{18,2},{3,19},{19,3},{4,20},{20... | collective-permute-start | bytes 3145736 | tf_op jit(solution)/shard_map/ppermute | solution.py:135
  224.5 191.6 %reduce-scatter.9.cloned.1.call-start = ((), (), s32[]{:S(2)}) async-start(), calls=%async_computation.6 | async-start | bytes 2228224 | tf_op jit(solution)/shard_map/reduce_scatter | solution.py:162
  224.5 22.6 %collective-permute-start.5 = (f32[512,512]{1,0:T(8,128)S(1)}, f32[512,512]{1,0:T(8,128)S(1)}, u32[]{:S(2)}, u32[]{:S(2)}) collective-permute-start(f32[512,512]{1,0:T(8,128)S(1)} %get-tuple-element.11), channel_id=1, source_target_pairs={{0,16},{16,0},{1,17},{17,1},{2,18},{18,2},{3,19},{19,3},{4,20},{20... | collective-permute-start | bytes 3145736 | tf_op jit(solution)/shard_map/ppermute | solution.py:135
  255.1 160.9 %copy-start.11 = (f32[1,64,2048]{2,1,0:T(8,128)S(1)}, f32[1,64,2048]{2,1,0:T(8,128)}, u32[]{:S(2)}) copy-start(f32[1,64,2048]{2,1,0:T(8,128)} %param.17) | copy-start | bytes 1572868
  255.2 236.2 %all-gather.3.cloned.1.call-start = ((), (), s32[]{:S(2)}) async-start(), calls=%async_computation.8 | async-start | bytes 8912896 | tf_op jit(solution)/shard_map/all_gather | solution.py:145
  255.8 162.3 %collective-permute-start = (f32[512,1024]{1,0:T(8,128)}, f32[512,1024]{1,0:T(8,128)}, u32[]{:S(2)}, u32[]{:S(2)}) collective-permute-start(f32[512,1024]{1,0:T(8,128)} %get-tuple-element.13), channel_id=1, source_target_pairs={{0,16},{16,0},{1,17},{17,1},{2,18},{18,2},{3,19},{19,3},{4,20},{20... | collective-permute-start | bytes 6291464 | tf_op jit(solution)/shard_map/ppermute | solution.py:135
  418.1 84.0 %copy-start.3 = (f32[1,512,1024]{2,1,0:T(8,128)S(1)}, f32[1,512,1024]{2,1,0:T(8,128)}, u32[]{:S(2)}) copy-start(f32[1,512,1024]{2,1,0:T(8,128)} %param.12) | copy-start | bytes 6291460
  491.3 10.8 %copy-start.8 = (f32[1,512,2048]{2,1,0:T(8,128)S(1)}, f32[1,512,2048]{2,1,0:T(8,128)}, u32[]{:S(2)}) copy-start(f32[1,512,2048]{2,1,0:T(8,128)} %param.14) | copy-start | bytes 12582916
Sparse Core Ops, SparseCore 0:
  159.4 63.1 reduce-scatter.4
  226.3 60.7 reduce-scatter.6
  290.8 60.7 reduce-scatter.10
  355.2 60.7 reduce-scatter.8
  418.1 73.2 all-gather.2
